TPU v7x, 128 devices: a whole 4x4x4 slice. The times are simulated.
128 devices in a mesh: latent: 16 (over z, y), row: 2 (over x_hi), col: 4 (over x_lo, core).
Axes of the slice: x: 4 (x_hi: 2, x_lo: 2; x = x_hi * 2 + x_lo), y: 4, z: 4, core: 2. Of those that a mesh axis runs over, the one named last changes fastest.
Arguments:
- observations: bfloat16 [128, 64, 2048], P('col', 'latent', 'row'), may hold values from -6 to 6
- rotation: float32 [64, 16], replicated, may hold values from -0.75 to 0.75
- ordering: int32 [2048], P('row'), may hold values from 0 to 2047, as said below
- working: bfloat16 [16, 2048, 2048], P('latent', 'row', 'col'), as said below
- factor_inverse: bfloat16 [16, 2, 512, 512], P('latent'), as said below
- panel_index: int32 [2], replicated, may hold values from 0 to 3
Outputs:
- trailing: float32 [16, 2048, 2048], P('latent', 'row', 'col')
- panels: bfloat16 [16, 2, 2048, 512], P('latent', None, 'row', 'col')
- whitened: float32 [16, 128, 2048], P('latent', 'col', 'row')
Inputs may be any that keep to these rules, and one draw needn't show every extreme that they name: `ordering`: a permutation of the stations that maps each block of 1024 consecutive positions onto the same block. `working`: symmetric in its last two dimensions. `factor_inverse`: lower triangular in its last two dimensions, with a positive diagonal.
All inputs are finite; a program needn't handle non-finite values.
Results may differ from a plain program's by a relative error of at most 0.0047.
Values may be sent and summed in bfloat16 or wider, within the bound.
A program may use at most 64 MiB of HBM per device.

v0:
```python
import functools

import jax
import jax.numpy as jnp
from jax import lax
from jax.experimental import pallas as pl
from jax.experimental.pallas import tpu as pltpu
from jax.sharding import PartitionSpec as P

MESH = pl.DeviceIdType.MESH
F32 = jnp.float32
BF16 = jnp.bfloat16
NB = 512
HALF = 1024
PER = 8
CH = NB // PER
TILE = 256


def nt(a, b):
    return lax.dot_general(a, b, (((1,), (1,)), ((), ())), preferred_element_type=F32)


def nn(a, b):
    return jnp.dot(a, b, preferred_element_type=F32)


def split(value):
    high = value.astype(BF16)
    return high, (value - high.astype(F32)).astype(BF16)


def aligned(index, unit):
    return pl.ds(pl.multiple_of(index * unit, unit), unit)


def loop(start, stop, action):
    def step(i, carry):
        action(i)
        return carry

    lax.fori_loop(start, stop, step, 0)


def kernel(
    halves, equal, lat,
    which, obs, rot_hbm, order_hbm, w_hbm, inv_hbm,
    trail, pans, white,
    inv, ww, b, bo, f, fs, x, xf, y, z, zf, pm, field, solved, rot, order,
    lsem, swap, rsem, bsem, osem, gsem, vsem, hold, pair, down, osend, gsend, gpass, vsend,
    s1, r1, s2, r2,
):
    h0, h1 = halves
    same = h0 == h1
    moved = (0,) if equal else (0, 1)
    last = moved[-1]
    lid = lax.axis_index("latent")
    r = lax.axis_index("row")
    c = lax.axis_index("col")
    xl = c // 2
    core = c % 2
    mate = 2 * xl + 1 - core
    odd = [(which[p] & 1).astype(F32) for p in range(2)]
    steps = obs.shape[0] // lat
    local_vars = obs.shape[1]
    turned = jnp.where(r == h1, 1.0, 0.0) * odd[1]

    def choose(low, high, weight):
        mix = jnp.full(low.shape, weight, F32).astype(low.dtype)
        return low * (1 - mix) + high * mix

    def remote(src, dst, send, recv, row, col):
        return pltpu.make_async_remote_copy(
            src_ref=src, dst_ref=dst, send_sem=send, recv_sem=recv,
            device_id={"row": row, "col": col}, device_id_type=MESH,
        )

    def arrived(ref, sem):
        pltpu.make_async_copy(ref, ref, sem).wait()

    def chunk(p, s, base=0):
        return b.at[p, pl.ds(pl.multiple_of(base + s * CH, CH), CH), :]

    loads = [
        pltpu.make_async_copy(w_hbm.at[0], ww.at[core], lsem.at[0]),
        pltpu.make_async_copy(inv_hbm.at[0], inv, lsem.at[1]),
        pltpu.make_async_copy(obs.at[pl.ds(lid * steps, steps)], x.at[lid], lsem.at[2]),
        pltpu.make_async_copy(rot_hbm, rot, lsem.at[3]),
        pltpu.make_async_copy(order_hbm, order, lsem.at[4]),
    ]
    loads[0].start()
    for load in loads[1:]:
        load.start()

    barrier = pltpu.get_barrier_semaphore()

    def greet(d):
        pl.semaphore_signal(
            barrier, inc=1, device_id={"latent": lax.rem(lid + d, lat)}, device_id_type=MESH
        )

    def greet_group(d):
        other = lax.rem(r * 4 + c + d, 8)
        pl.semaphore_signal(
            barrier, inc=1, device_id={"row": other // 4, "col": other % 4}, device_id_type=MESH
        )

    loop(1, lat, greet)
    loop(1, 8, greet_group)
    pl.semaphore_wait(barrier, lat - 1 + 7)

    swapper = (xl == h0) | (xl == h1)

    def swapping(s):
        at = aligned(s, CH)
        return remote(
            w_hbm.at[0, at, :], ww.at[core, at, :], swap.at[0, s], swap.at[1, s], r, mate
        )

    def swapped(s):
        arrived(ww.at[1 - core, aligned(s, CH), :], swap.at[1, s])

    @pl.when(swapper)
    def _():
        def needed(u):
            swapping(2 * u + 1 - core).start()
            swapping(2 * u + 1 - core + PER).start()

        def others(u):
            swapping(2 * u + core).start()
            swapping(2 * u + core + PER).start()

        loop(0, PER // 2, needed)
        loop(0, PER // 2, others)

    def first(d):
        to = lax.rem(lid + d, lat)
        return pltpu.make_async_remote_copy(
            src_ref=obs.at[pl.ds(to * steps, steps)], dst_ref=x.at[lid],
            send_sem=s1.at[d], recv_sem=r1.at[d],
            device_id={"latent": to}, device_id_type=MESH,
        )

    def second(d):
        to = lax.rem(lid + d, lat)
        return pltpu.make_async_remote_copy(
            src_ref=y.at[to], dst_ref=z.at[lid],
            send_sem=s2.at[d], recv_sem=r2.at[d],
            device_id={"latent": to}, device_id_type=MESH,
        )

    loop(1, lat, lambda d: first(d).start())
    loads[0].wait()

    def holding(p, t):
        s = 2 * t + core
        return remote(chunk(p, s), chunk(p, s), hold.at[p, t], rsem.at[p, s], r, 2 * (1 - xl) + core)

    def stage(p, s):
        at = aligned(s, CH)
        value = choose(ww[0, at, :], ww[1, at, :], odd[p])
        if p == 0 and not same:
            flip = aligned((s + PER) % (2 * PER), CH)
            value = choose(value, choose(ww[0, flip, :], ww[1, flip, :], odd[p]), turned)
        b[p, at, :] = value

    def stage_all(s):
        for p in moved:
            @pl.when(xl == halves[p])
            def _():
                stage(p, s)

    def hold_all(t):
        for p in moved:
            @pl.when(xl == halves[p])
            def _():
                holding(p, t).start()

    @pl.when(swapper)
    def _():
        def early(u):
            swapped(2 * u + core)
            swapped(2 * u + core + PER)
            stage_all(2 * u + core)

            @pl.when(u > 0)
            def _():
                hold_all(u - 1)

        def late(t):
            stage_all(2 * t + core)
            hold_all(t - 1)

        loop(0, PER // 2, early)
        loop(PER // 2, PER, late)
        hold_all(PER - 1)

        def finish_swap(t):
            swapped(2 * t + 1 - core)

        loop(0, PER, finish_swap)
        loop(0, PER, lambda t: stage_all(2 * t + 1 - core))

    for load in loads[1:]:
        load.wait()

    is_n = (r == h0) & (xl == 1 - h0)
    source = (r == h1) & (xl == h1)
    sink = (r == 1 - h1) & (xl == 1 - h1)
    swing = (r == 1 - h1) & (xl == h1)
    g_at = pl.ds(HALF + NB, NB)
    bc_at = pl.ds(HALF, NB)

    def across(t):
        s = 2 * t + core
        src = chunk(0, s, HALF + NB) if same else chunk(0, s)
        return remote(
            src, chunk(0, s, HALF + NB), gsend.at[t], gsem.at[s], 1 - h1, 2 * (1 - h1) + core
        )

    def pick_own():
        if same:
            b[0, g_at, :] = choose(b[0, :NB, :], b[0, NB:HALF, :], odd[1])
        else:
            b[0, g_at, :] = b[0, :NB, :]

    if same:
        @pl.when(source)
        def _():
            pick_own()
            loop(0, PER // 2, lambda t: across(t).start())

    def swing_out(u):
        return remote(
            chunk(0, u, HALF), bo.at[aligned(u, CH), :], osend.at[u], osem.at[u], r, mate
        )

    for p in moved:
        @pl.when((r == halves[p]) & (xl == 1 - halves[p]))
        def _():
            b[p, bc_at, :] = choose(ww[core, :NB, :], ww[core, NB:, :], odd[p]).T

    if not same:
        @pl.when(is_n)
        def _():
            loop(0, PER, lambda u: swing_out(u).start())

    left = pl.ds(0, NB)
    right = pl.ds(NB, NB)
    place = order[...] - r * HALF

    def permutation(i):
        at = lax.broadcasted_iota(jnp.int32, (128, HALF), 0) + i * 128
        pm[aligned(i, 128), :] = jnp.where(at == place, 1.0, 0.0).astype(BF16)

    loop(0, HALF // 128, permutation)

    mixed_rows = lat * steps
    depth = lat * steps * local_vars
    total_vars = lat * local_vars
    pick_latent = (
        lax.broadcasted_iota(jnp.int32, (mixed_rows, lat), 0) // steps
        == lax.broadcasted_iota(jnp.int32, (mixed_rows, lat), 1)
    )
    pick_latent = jnp.where(pick_latent, 1.0, 0.0).astype(BF16)
    along = lax.broadcasted_iota(jnp.int32, (total_vars, depth), 1)
    pick_var = (along // (steps * local_vars)) * local_vars + along % local_vars
    pick_var = pick_var == lax.broadcasted_iota(jnp.int32, (total_vars, depth), 0)
    pick_var = jnp.where(pick_var, 1.0, 0.0).astype(BF16)
    wide = lax.broadcasted_iota(jnp.int32, (mixed_rows, depth), 1)
    tall = lax.broadcasted_iota(jnp.int32, (mixed_rows, depth), 0)
    same_step = (wide // local_vars) % steps == tall % steps

    def mixer(part):
        spread = nn(nn(pick_latent, part).astype(BF16), pick_var)
        return jnp.where(same_step, spread, 0.0).astype(BF16)

    rot_high, rot_low = split(rot[...])
    mix_high, mix_low = mixer(rot_high), mixer(rot_low)

    def to_mate(p, t):
        s = 2 * t + core
        return remote(chunk(p, s), chunk(p, s), pair.at[p, t], rsem.at[p, s], r, mate)

    def to_down(p, t):
        s = 2 * t + core
        return remote(
            chunk(p, s), chunk(p, s % PER, HALF), down.at[p, t], bsem.at[p, s % PER],
            1 - halves[p], 2 * halves[p] + s // PER,
        )

    def product(rows, p):
        near = nt(rows[:, : NB // 2], inv[p, : NB // 2, : NB // 2])
        far = nt(rows, inv[p, NB // 2 :, :])
        return near.astype(BF16), far.astype(BF16)

    def take_step(t):
        @pl.when(xl == 1 - h0)
        def _():
            s = 2 * t + 1 - core
            arrived(chunk(0, s), rsem.at[0, s])

        at = aligned(t, 2 * CH)
        near, far = product(b[0, at, :], 0)
        fs[at, : NB // 2] = near
        fs[at, NB // 2 :] = far

    def relay(t):
        pass_on(t)

        @pl.when(t > 0)
        def _():
            take_step(t - 1)

    def pass_on(t):
        s = 2 * t + core
        for p in moved:
            @pl.when(xl == 1 - halves[p])
            def _():
                arrived(chunk(p, s), rsem.at[p, s])
                to_mate(p, t).start()

                @pl.when(r == halves[p])
                def _():
                    to_down(p, t).start()

                if p == 0 and not same:
                    @pl.when((r == h1) & (t < PER // 2))
                    def _():
                        across(t).start()

    loop(0, 2, relay)
    loop(1, lat, lambda d: first(d).wait_recv())
    for i in range(lat):
        for t in range(steps):
            xf[pl.ds((i * steps + t) * local_vars, local_vars), :] = x[i, t].astype(F32)
    samples = xf[...].astype(BF16)
    mixed = nn(mix_high, samples) + nn(mix_low, samples)
    for i in range(lat):
        y[i] = mixed[i * steps : (i + 1) * steps]
    loop(1, lat, lambda d: second(d).start())
    own_z = pltpu.make_async_copy(y.at[lid], z.at[lid], lsem.at[5])
    own_z.start()
    loop(2, 5, relay)
    own_z.wait()
    loop(1, lat, lambda d: second(d).wait_recv())
    for i in range(lat):
        zf[pl.ds(i * steps, steps), :] = z[i]
    high, low = split(zf[...])
    field[...] = nn(high, pm[...]) + nn(low, pm[...])

    def solve(p):
        part = choose(field[:, :NB], field[:, NB:], odd[p])
        if p == 1:
            part = part - nt(solved[0], f[g_at, left])
        top, rest = split(part)
        solved[p] = (nt(top, inv[p]) + nt(rest, inv[p])).astype(BF16)

    def sharing(p):
        return remote(solved.at[p], solved.at[p], vsend.at[p], vsem.at[p], 1 - halves[p], c)

    def share(p):
        @pl.when(r == halves[p])
        def _():
            solve(p)
            sharing(p).start()

    def receive(p):
        @pl.when(r != halves[p])
        def _():
            arrived(solved.at[p], vsem.at[p])

    share(0)
    loop(5, PER, relay)
    take_step(PER - 1)

    if not equal:
        @pl.when(xl == 1 - h1)
        def _():
            def other(t):
                s = 2 * t + 1 - core
                arrived(chunk(1, s), rsem.at[1, s])

            loop(0, PER, other)

    for p in moved:
        @pl.when(r == xl)
        def _():
            own = b[p, aligned(core, NB), :]
            if p == 0 and not same:
                own = choose(own, b[p, aligned(1 - core, NB), :], turned)
            b[p, bc_at, :] = own

        @pl.when((r == 1 - halves[p]) & (xl == halves[p]))
        def _():
            def below(u):
                arrived(chunk(p, u, HALF), bsem.at[p, u])
                if p == 0 and same:
                    swing_out(u).start()

            loop(0, PER, below)

    if not same:
        @pl.when(r == h1)
        def _():
            pick_own()
    else:
        @pl.when((r == h1) & (xl == 1 - h1))
        def _():
            pick_own()

    def sink_pass(t):
        s = 2 * t + core
        return remote(
            chunk(0, s, HALF + NB), chunk(0, s, HALF + NB), gpass.at[t], gsem.at[s], r, mate
        )

    @pl.when(sink)
    def _():
        def take(t):
            s = 2 * t + core
            arrived(chunk(0, s, HALF + NB), gsem.at[s])
            sink_pass(t).start()

        def rest(t):
            s = 2 * t + 1 - core
            arrived(chunk(0, s, HALF + NB), gsem.at[s])

        loop(0, PER // 2, take)
        loop(0, PER // 2, rest)

    @pl.when(swing)
    def _():
        def gather(u):
            arrived(bo.at[aligned(u, CH), :], osem.at[u])

        loop(0, PER, gather)
        even_core = jnp.where(core == 0, 1.0, 0.0)
        b[0, g_at, :] = choose(
            b[0, bc_at, :], bo[...], even_core * odd[1] + (1 - even_core) * (1 - odd[1])
        )

    def keep(p, at, pieces):
        f[at, pl.ds(p * NB, NB // 2)] = pieces[0]
        f[at, pl.ds(p * NB + NB // 2, NB // 2)] = pieces[1]

    def first_factor(i):
        at = aligned(i, TILE)
        keep(0, at, product(b[0, at, :], 0))

    loop(HALF // TILE, 2 * HALF // TILE, first_factor)

    def settle(i):
        at = aligned(i, TILE)
        rows = fs[at, :]
        if not same:
            rows = choose(rows, fs[aligned((i + 2) % 4, TILE), :], turned)
        f[at, left] = rows

    loop(0, HALF // TILE, settle)

    def second_factor(i):
        at = aligned(i, TILE)
        part = b[last, at, :].astype(F32) - nt(f[at, left], f[g_at, left])
        keep(1, at, product(part.astype(BF16), 1))

    receive(0)
    share(1)
    loop(0, 3 * NB // TILE, second_factor)

    mine = pl.ds(pl.multiple_of(c * 128, 128), 128)
    mine_after = pl.ds(pl.multiple_of(c * 128 + NB, 128), 128)

    def finish(m):
        at = aligned(m, TILE)
        trail[0, at, :] = ww[core, at, :].astype(F32) - nt(f[at, :], f[bc_at, :])
        pans[0, 0, at, :] = f[at, mine]
        pans[0, 1, at, :] = f[at, mine_after]

    loop(0, HALF // TILE, finish)
    receive(1)

    def whiten(m):
        at = aligned(m, TILE)
        white[0, :, at] = field[:, at] - (
            nt(solved[0], f[at, left]) + nt(solved[1], f[at, right])
        )

    loop(0, HALF // TILE, whiten)

    @pl.when(swapper)
    def _():
        loop(0, 2 * PER, lambda s: swapping(s).wait_send())

    for p in moved:
        @pl.when(xl == halves[p])
        def _():
            loop(0, PER, lambda t: holding(p, t).wait_send())

        @pl.when(xl == 1 - halves[p])
        def _():
            loop(0, PER, lambda t: to_mate(p, t).wait_send())

            @pl.when(r == halves[p])
            def _():
                loop(0, PER, lambda t: to_down(p, t).wait_send())

    for p in range(2):
        @pl.when(r == halves[p])
        def _():
            sharing(p).wait_send()

    @pl.when(source)
    def _():
        loop(0, PER // 2, lambda t: across(t).wait_send())

    @pl.when(sink)
    def _():
        loop(0, PER // 2, lambda t: sink_pass(t).wait_send())

    @pl.when(swing)
    def _():
        loop(0, PER, lambda u: swing_out(u).wait_send())

    loop(1, lat, lambda d: first(d).wait_send())
    loop(1, lat, lambda d: second(d).wait_send())


def solution(mesh):
    lat = mesh.shape["latent"]

    def local(observations, rotation, ordering, working, factor_inverse, panel_index):
        times, local_vars, stations = observations.shape
        steps = times // lat
        vmem = pl.BlockSpec(memory_space=pltpu.VMEM)
        anyw = pl.BlockSpec(memory_space=pl.ANY)
        dma = pltpu.SemaphoreType.DMA

        def call(halves, equal, *operands):
            return pl.pallas_call(
                functools.partial(kernel, halves, equal, lat),
                out_shape=(
                    jax.ShapeDtypeStruct((1, HALF, NB), F32),
                    jax.ShapeDtypeStruct((1, 2, HALF, 128), BF16),
                    jax.ShapeDtypeStruct((1, times, HALF), F32),
                ),
                in_specs=[pl.BlockSpec(memory_space=pltpu.SMEM)] + [anyw] * 5,
                out_specs=(vmem, vmem, vmem),
                scratch_shapes=[
                    pltpu.VMEM((2, NB, NB), BF16),
                    pltpu.VMEM((2, HALF, NB), BF16),
                    pltpu.VMEM((2, 2 * HALF, NB), BF16),
                    pltpu.VMEM((NB, NB), BF16),
                    pltpu.VMEM((2 * HALF, 2 * NB), BF16),
                    pltpu.VMEM((HALF, NB), BF16),
                    pltpu.VMEM((lat, steps, local_vars, HALF), BF16),
                    pltpu.VMEM((times * local_vars, HALF), F32),
                    pltpu.VMEM((lat, steps, HALF), F32),
                    pltpu.VMEM((lat, steps, HALF), F32),
                    pltpu.VMEM((times, HALF), F32),
                    pltpu.VMEM((HALF, HALF), BF16),
                    pltpu.VMEM((times, HALF), F32),
                    pltpu.VMEM((2, times, NB), BF16),
                    pltpu.VMEM(rotation.shape[::-1], F32),
                    pltpu.VMEM((1, HALF), jnp.int32),
                    dma((6,)),
                    dma((2, 2 * PER)),
                    dma((2, 2 * PER)),
                    dma((2, PER)),
                    dma((PER,)),
                    dma((PER,)),
                    dma((2,)),
                    dma((2, PER)),
                    dma((2, PER)),
                    dma((2, PER)),
                    dma((PER,)),
                    dma((PER // 2,)),
                    dma((PER // 2,)),
                    dma((2,)),
                    dma((lat,)),
                    dma((lat,)),
                    dma((lat,)),
                    dma((lat,)),
                ],
                compiler_params=pltpu.CompilerParams(
                    collective_id=4 + halves[0] if equal else halves[0] * 2 + halves[1], has_side_effects=True,
                    vmem_limit_bytes=48 << 20,
                ),
                name=f"panels_{halves[0]}{halves[1]}{int(equal)}",
            )(*operands)

        branches = [functools.partial(call, (i, j), False) for i in range(2) for j in range(2)]
        branches += [functools.partial(call, (i, i), True) for i in range(2)]
        code = jnp.sum(panel_index * jnp.array([4, 1], jnp.int32))
        upper, lower = code >> 3, (code >> 1) & 1
        choice = jnp.where(lax.rem(code, 5) == 0, 4 + upper, upper * 2 + lower)
        return lax.switch(
            choice, branches,
            panel_index, observations, rotation.T, ordering.reshape(1, HALF), working,
            factor_inverse,
        )

    return jax.shard_map(
        local,
        mesh=mesh,
        in_specs=(
            P("col", "latent", "row"),
            P(),
            P("row"),
            P("latent", "row", "col"),
            P("latent", None, None, None),
            P(),
        ),
        out_specs=(
            P("latent", "row", "col"),
            P("latent", None, "row", "col"),
            P("latent", "col", "row"),
        ),
        check_vma=False,
    )
```

profile of v0, /device:TPU:3, one launch (start us, length us, event | category | flops | bytes accessed | tf_op | source)
XLA Modules:
  0.0 43.3 jit_solution(10755777214542058371)
XLA Ops:
  0.6 1.3 %multiply_reduce_fusion = s32[]{:T(128)} fusion(s32[2]{0:T(128)} %param.18, s32[2]{0:T(128)} %constant.14.clone), kind=kLoop, calls=%fused_computation | loop fusion | flops 3 | bytes 20 | tf_op jit(solution)/shard_map/reduce_sum | solution.py:594
  3.9 36.6 %conditional.1 = ((f32[1,1024,512]{2,1,0:T(8,128)S(1)}, bf16[1,2,1024,128]{3,2,1,0:T(8,128)(2,1)S(1)}, f32[1,32,1024]{2,1,0:T(8,128)S(1)})) conditional(s32[]{:T(128)} %clamp.3, (s32[2]{0:T(128)}, bf16[32,4,1024]{2,1,0:T(4,128)(2,1)}, f32[16,64]{1,0:T(8,128)}, s32[1024]{0:T(1024)}, bf16[1,1024,512]{2,1,0:T(8,128)(2,1)}, ...), branch_computations={%region_1.2_spmd, %region_2.3_spmd, %region_3.4_spmd, %region_4.5_... | conditional | bytes 8 | solution.py:597
  3.9 36.4 %panels_010.1 = (f32[1,1024,512]{2,1,0:T(8,128)S(1)}, bf16[1,2,1024,128]{3,2,1,0:T(8,128)(2,1)S(1)}, f32[1,32,1024]{2,1,0:T(8,128)S(1)}) custom-call(s32[2]{0:T(128)} %get-tuple-element.78.which, bf16[32,4,1024]{2,1,0:T(4,128)(2,1)} %get-tuple-element.157.obs, f32[16,64]{1,0:T(8,128)} %get-tuple-element.80.rot_hbm, s32[1,1024]{1,0:T(1,128)} %bitcast.14, ...), custom_call_target="tpu_custom_call" | custom-call | tf_op jit(solution)/shard_map/cond/branch_1_fun/panels_010/pallas_call | solution.py:540
  40.6 1.3 %copy.73 = f32[1,1024,512]{2,1,0:T(8,128)} copy(f32[1,1024,512]{2,1,0:T(8,128)S(1)} %get-tuple-element.207) | data formatting | bytes 4194304
  41.9 0.8 %copy.74 = bf16[1,2,1024,128]{3,2,1,0:T(8,128)(2,1)} copy(bf16[1,2,1024,128]{3,2,1,0:T(8,128)(2,1)S(1)} %get-tuple-element.208) | data formatting | bytes 1048576
  42.7 0.7 %copy.75 = f32[1,32,1024]{2,1,0:T(8,128)} copy(f32[1,32,1024]{2,1,0:T(8,128)S(1)} %get-tuple-element.209) | data formatting | bytes 262144
where the time goes:
time: 43.6 us; the launch traced here: 43.3 us
  Pallas kernels  36.4 us (83%)
  local copies, waits for them, and re-layouts  2.77 us (6%)
  between operations  2.6 us (6%)
  other arithmetic  1.31 us (3%)
    pallas_call x1, Pallas kernels, call(): pl.pallas_call(functools.partial(kernel, halves, equal, lat), out_shape=(...  36.4 us
    unnamed x3, local copies, waits for them, and re-layouts  2.77 us
    reduce_sum x1, other arithmetic, local(): code = jnp.sum(panel_index * jnp.array([4, 1], jnp.int32))  1.31 us

commit v1 on v0

--- a/solution.py
+++ b/solution.py
@@ -14,7 +14,7 @@
 HALF = 1024
 PER = 8
 CH = NB // PER
-TILE = 256
+TILE = 512
 
 
 def nt(a, b):
@@ -300,10 +300,12 @@
             s = 2 * t + 1 - core
             arrived(chunk(0, s), rsem.at[0, s])
 
-        at = aligned(t, 2 * CH)
-        near, far = product(b[0, at, :], 0)
-        fs[at, : NB // 2] = near
-        fs[at, NB // 2 :] = far
+        @pl.when(t % 2 == 1)
+        def _():
+            at = aligned(t // 2, 4 * CH)
+            near, far = product(b[0, at, :], 0)
+            fs[at, : NB // 2] = near
+            fs[at, NB // 2 :] = far
 
     def relay(t):
         pass_on(t)
@@ -454,7 +456,7 @@
         at = aligned(i, TILE)
         rows = fs[at, :]
         if not same:
-            rows = choose(rows, fs[aligned((i + 2) % 4, TILE), :], turned)
+            rows = choose(rows, fs[aligned((i + NB // TILE) % (HALF // TILE), TILE), :], turned)
         f[at, left] = rows
 
     loop(0, HALF // TILE, settle)

time: 43.6 us -> 43.3 us (level)
  Pallas kernels: 36.4 us -> 35.9 us
    pallas_call x1, Pallas kernels: 36.4 us -> 35.9 us  [call(): pl.pallas_call(functools.partial(kernel, halves, equal, lat), out_shape=(...]
where the time goes in v1:
time: 43.3 us; the launch traced here: 43.2 us
  Pallas kernels  35.9 us (83%)
  local copies, waits for them, and re-layouts  2.77 us (6%)
  between operations  2.6 us (6%)
  other arithmetic  1.31 us (3%)
  loops' own time  0.57 us (1%)
    pallas_call x1, Pallas kernels, call(): pl.pallas_call(functools.partial(kernel, halves, equal, lat), out_shape=(...  35.9 us
    unnamed x3, local copies, waits for them, and re-layouts  2.77 us
    reduce_sum x1, other arithmetic, local(): code = jnp.sum(panel_index * jnp.array([4, 1], jnp.int32))  1.31 us

profile of v1, /device:TPU:3, one launch (start us, length us, event | category | flops | bytes accessed | tf_op | source)
XLA Modules:
  0.0 43.2 jit_solution(857950046663790413)
XLA Ops:
  0.6 1.3 %multiply_reduce_fusion = s32[]{:T(128)} fusion(s32[2]{0:T(128)} %param.18, s32[2]{0:T(128)} %constant.14.clone), kind=kLoop, calls=%fused_computation | loop fusion | flops 3 | bytes 20 | tf_op jit(solution)/shard_map/reduce_sum | solution.py:596
  3.9 36.5 %conditional.1 = ((f32[1,1024,512]{2,1,0:T(8,128)S(1)}, bf16[1,2,1024,128]{3,2,1,0:T(8,128)(2,1)S(1)}, f32[1,32,1024]{2,1,0:T(8,128)S(1)})) conditional(s32[]{:T(128)} %clamp.3, (s32[2]{0:T(128)}, bf16[32,4,1024]{2,1,0:T(4,128)(2,1)}, f32[16,64]{1,0:T(8,128)}, s32[1024]{0:T(1024)}, bf16[1,1024,512]{2,1,0:T(8,128)(2,1)}, ...), branch_computations={%region_1.2_spmd, %region_2.3_spmd, %region_3.4_spmd, %region_4.5_... | conditional | bytes 8 | solution.py:599
  3.9 35.9 %panels_100.1 = (f32[1,1024,512]{2,1,0:T(8,128)S(1)}, bf16[1,2,1024,128]{3,2,1,0:T(8,128)(2,1)S(1)}, f32[1,32,1024]{2,1,0:T(8,128)S(1)}) custom-call(s32[2]{0:T(128)} %get-tuple-element.84.which, bf16[32,4,1024]{2,1,0:T(4,128)(2,1)} %get-tuple-element.158.obs, f32[16,64]{1,0:T(8,128)} %get-tuple-element.86.rot_hbm, s32[1,1024]{1,0:T(1,128)} %bitcast.15, ...), custom_call_target="tpu_custom_call" | custom-call | tf_op jit(solution)/shard_map/cond/branch_2_fun/panels_100/pallas_call | solution.py:542
  40.4 1.3 %copy.73 = f32[1,1024,512]{2,1,0:T(8,128)} copy(f32[1,1024,512]{2,1,0:T(8,128)S(1)} %get-tuple-element.207) | data formatting | bytes 4194304
  41.7 0.8 %copy.74 = bf16[1,2,1024,128]{3,2,1,0:T(8,128)(2,1)} copy(bf16[1,2,1024,128]{3,2,1,0:T(8,128)(2,1)S(1)} %get-tuple-element.208) | data formatting | bytes 1048576
  42.5 0.7 %copy.75 = f32[1,32,1024]{2,1,0:T(8,128)} copy(f32[1,32,1024]{2,1,0:T(8,128)S(1)} %get-tuple-element.209) | data formatting | bytes 262144
